TPU v7x, 32 devices: a whole 2x2x4 slice. The times are simulated.
32 devices in a mesh: grp: 2 (over y), tm: 4 (over z), tmpl: 2 (over x), chan: 2 (over core).
Axes of the slice: x: 2, y: 2, z: 4, core: 2. Of those that a mesh axis runs over, the one named last changes fastest.
Arguments:
- record: bfloat16 [32, 4096], P('chan', ('grp', 'tm')), parts along dimension 1, may hold values from -640 to 640
- templates: bfloat16 [2, 768, 32, 512], P('tmpl', 'tm', 'chan'), may hold values from -0.046875 to 0.046875
- span_list: int32 [8, 4], P(('grp', 'tm')), parts along dimension 0, may hold values from -1 to 3, as said below
Outputs:
- scan_out: float32 [1536, 4096], P(('tmpl', 'chan'), ('grp', 'tm')), parts along dimension 1
There are 2 independent parts, one for each index of `grp`. A program takes and returns all parts, laid end to end along the dimension named above; an argument that names none is the same for every part. Nothing has to cross between parts.
Inputs may be any that keep to these rules, and one draw needn't show every extreme that they name: `span_list`: each shard lists distinct blocks in its first slots and -1 in the rest; between 1 and 4 blocks a shard, exactly 8 in all shards together, and some shard lists 4.
All inputs are finite; a program needn't handle non-finite values.
Results may differ from a plain program's by a relative error of at most 0.0003.
Values may be sent and summed in bfloat16 or wider, within the bound.
A program may use at most 64 MiB of HBM per device.

v0:
```python
import jax
import jax.numpy as jnp
from jax import lax
from jax.sharding import PartitionSpec as P

C = 32
L = 512
SPAN = 128
MOST_DENSE = 4


def from_behind(block, axis, distance):
    devices = range(lax.axis_size(axis))
    route = [(i - distance, i) for i in devices if i - distance in devices]
    return lax.ppermute(block, axis, route)


def windows(segment):
    seg_len = segment.shape[1]
    tiled = jnp.tile(segment, (1, SPAN + 1))
    flattened = tiled[:, : SPAN * (seg_len + 1)]
    return flattened.reshape(segment.shape[0], SPAN, seg_len + 1)[:, :, :L]


def slot_windows(extended, own_list):
    stacked = []
    for slot in range(MOST_DENSE):
        span_at = own_list[slot]
        segment = lax.dynamic_slice_in_dim(extended, jnp.maximum(span_at, 0) * SPAN, SPAN + L, 1)
        stacked.append(jnp.where(span_at >= 0, windows(segment), jnp.zeros((), extended.dtype)))
    return jnp.stack(stacked)


def local(record, templates, span_list):
    own_list = span_list[0]
    following = from_behind(record, "tm", -1)
    extended = jnp.concatenate([record, following], axis=1)
    own_windows = slot_windows(extended, own_list)
    product = jnp.einsum(
        "kcl,qcrl->kqr",
        lax.all_gather(templates, "tm", axis=1, tiled=True)[0],
        own_windows,
        preferred_element_type=jnp.float32,
    )
    product = product.reshape(product.shape[0], MOST_DENSE * SPAN)
    summed = lax.psum_scatter(product, "chan", scatter_dimension=0, tiled=True)
    local_energy = jnp.sum(jnp.square(own_windows.astype(jnp.float32)), axis=(1, 3)).reshape(-1)
    energy = lax.psum(local_energy, "chan")
    return summed * lax.rsqrt(energy / (C * L) + 1e-05)[None, :]


def solution(mesh):
    in_specs = (P("chan", ("grp", "tm")), P("tmpl", "tm", "chan", None), P(("grp", "tm"), None))
    out_specs = P(("tmpl", "chan"), ("grp", "tm"))
    return jax.shard_map(local, mesh=mesh, in_specs=in_specs, out_specs=out_specs, check_vma=False)
```

profile of v0, /device:TPU:0, one launch (start us, length us, event | category | flops | bytes accessed | tf_op | source)
XLA Modules:
  0.0 266.6 jit_solution(5071008891932363301)
XLA Ops:
  6.5 0.0 all-gather.2.cloned.1.call-start
  6.5 5.3 %copy.6 = bf16[1,192,16,512]{3,1,2,0:T(8,128)(2,1)} copy(bf16[1,192,16,512]{3,2,1,0:T(8,128)(2,1)} %param.4) | data formatting | bytes 6291456 | tf_op args[1]
  11.8 0.0 copy-start.2
  11.8 0.0 copy-start.3
  11.8 0.0 all-gather.2.cloned.1.call-update
  11.8 0.0 reduce-scatter.2.cloned.1.call-start
  11.9 0.6 copy-done.2
  12.5 1.3 collective-permute-start
  13.8 0.0 copy-done.3
  13.8 0.7 fusion.7
  19.8 0.0 collective-permute-done
  19.8 0.2 tile.16
  20.0 0.3 copy.9
  20.4 0.2 slice.52
  20.6 8.1 %reshape.67 = bf16[16,128,641]{2,1,0:T(8,128)(2,1)} reshape(bf16[16,82048]{1,0:T(8,128)(2,1)S(1)} %slice.52) | data formatting | bytes 5251072 | tf_op jit(solution)/shard_map/reshape | solution.py:22
  28.6 0.2 tile.42
  28.9 0.3 copy.12
  29.2 0.2 slice.58
  29.4 7.9 %reshape.70 = bf16[16,128,641]{2,1,0:T(8,128)(2,1)} reshape(bf16[16,82048]{1,0:T(8,128)(2,1)S(1)} %slice.58) | data formatting | bytes 5251072 | tf_op jit(solution)/shard_map/reshape | solution.py:22
  37.3 0.2 tile.40
  37.5 0.3 copy.11
  37.8 0.2 slice.56
  38.0 7.9 %reshape.69 = bf16[16,128,641]{2,1,0:T(8,128)(2,1)} reshape(bf16[16,82048]{1,0:T(8,128)(2,1)S(1)} %slice.56) | data formatting | bytes 5251072 | tf_op jit(solution)/shard_map/reshape | solution.py:22
  45.9 0.2 tile.18
  46.1 0.3 copy.10
  46.4 0.2 slice.54
  46.6 8.1 %reshape.68 = bf16[16,128,641]{2,1,0:T(8,128)(2,1)} reshape(bf16[16,82048]{1,0:T(8,128)(2,1)S(1)} %slice.54) | data formatting | bytes 5251072 | tf_op jit(solution)/shard_map/reshape | solution.py:22
  54.7 0.0 copy-start
  54.7 0.0 copy-start.1
  54.7 4.1 %fusion.2 = (bf16[1,16,128,512]{3,2,1,0:T(8,128)(2,1)S(1)}, bf16[1,16,128,512]{3,2,1,0:T(8,128)(2,1)}) fusion(bf16[16,128,641]{2,1,0:T(8,128)(2,1)} %reshape.70, pred[]{:T(512)} %bitcast.9, bf16[16,128,641]{2,1,0:T(8,128)(2,1)} %reshape.69, pred[]{:T(512)} %bitcast.6), kind=kLoop, calls=%fused_computation.5 | loop fusion | flops 2097152 | bytes 8388610 | tf_op jit(solution)/shard_map/stack | solution.py:31
  58.8 0.0 copy-done
  58.8 0.8 copy-done.1
  59.7 2.2 fusion.4
  61.9 171.0 %all-gather.2.cloned.1.call-done = bf16[1,768,16,512]{3,1,2,0:T(8,128)(2,1)} async-done(((bf16[1,192,16,512]{3,1,2,0:T(8,128)(2,1)}), bf16[1,768,16,512]{3,1,2,0:T(8,128)(2,1)}) %all-gather.2.cloned.1.call-update) | async-done | bytes 12582928 | tf_op jit(solution)/shard_map/all_gather | solution.py:41
  232.9 14.3 %fusion = f32[4,128,768,1]{2,1,3,0:T(8,128)} fusion(bf16[1,768,16,512]{3,1,2,0:T(8,128)(2,1)} %all-gather.2.cloned.1.call-done, bf16[1,16,128,512]{3,2,1,0:T(8,128)(2,1)S(1)} %get-tuple-element.13, bf16[1,16,128,512]{3,2,1,0:T(8,128)(2,1)} %get-tuple-element.14, bf16[1,16,128,512]{3,2,1,0:T(8,128)(2,1)} %get-tuple-element.15, ...), kind=kOutput, calls=%fused_computation.1 | convolution fusion | flops 6455033856 | bytes 22544384 | tf_op jit(solution)/shard_map/kcl,qcrl->kqr/dot_general | solution.py:39
  247.2 3.0 %copy.7 = f32[768,512]{1,0:T(8,128)} copy(f32[768,512]{0,1:T(8,128)} %bitcast.43) | data formatting | bytes 3145728 | tf_op jit(solution)/shard_map/reshape | solution.py:45
  250.3 0.0 reduce-scatter.2.cloned.1.call-update
  250.3 4.3 %multiply_reduce_fusion = f32[4,128]{1,0:T(4,128)S(1)} fusion(bf16[1,16,128,512]{3,2,1,0:T(8,128)(2,1)S(1)} %get-tuple-element.13, bf16[1,16,128,512]{3,2,1,0:T(8,128)(2,1)} %get-tuple-element.14, bf16[1,16,128,512]{3,2,1,0:T(8,128)(2,1)} %get-tuple-element.15, bf16[1,16,128,512]{3,2,1,0:T(8,128)(2,1)} %get-tuple-element.16), kind=kLoop, calls=%fused_computation | loop fusion | flops 25165312 | bytes 8390656 | tf_op jit(solution)/shard_map/reduce_sum | solution.py:47
  254.6 2.5 psum.7
  257.1 0.6 reduce-scatter.2.cloned.1.call-done
  257.7 2.1 broadcast_multiply_fusion
  (4 shorter events, 0.0 us)
Async XLA Ops:
  6.5 226.4 %all-gather.2.cloned.1.call-start = ((), (), s32[]{:S(2)}) async-start(), calls=%async_computation.1 | async-start | bytes 15728640 | tf_op jit(solution)/shard_map/all_gather | solution.py:41
  11.8 0.7 copy-start.2
  11.8 2.0 copy-start.3
  11.8 245.8 %reduce-scatter.2.cloned.1.call-start = ((), (), s32[]{:S(2)}) async-start(), calls=%async_computation.2 | async-start | bytes 2359296 | tf_op jit(solution)/shard_map/reduce_scatter | solution.py:46
  12.5 7.2 %collective-permute-start = (bf16[16,512]{1,0:T(8,128)(2,1)S(1)}, bf16[16,512]{1,0:T(8,128)(2,1)S(1)}, u32[]{:S(2)}, u32[]{:S(2)}) collective-permute-start(bf16[16,512]{1,0:T(8,128)(2,1)S(1)} %copy-done.2), channel_id=1, source_target_pairs={{4,0},{8,4},{12,8},{5,1},{9,5},{13,9},{6,2},{10,6},{14,10},{7,3},{... | collective-permute-start | bytes 49160 | tf_op jit(solution)/shard_map/ppermute | solution.py:15
  54.7 4.1 %copy-start = (bf16[16,128,641]{2,1,0:T(8,128)(2,1)S(1)}, bf16[16,128,641]{2,1,0:T(8,128)(2,1)}, u32[]{:S(2)}) copy-start(bf16[16,128,641]{2,1,0:T(8,128)(2,1)} %reshape.67) | copy-start | bytes 7876612
  54.7 4.9 %copy-start.1 = (bf16[16,128,641]{2,1,0:T(8,128)(2,1)S(1)}, bf16[16,128,641]{2,1,0:T(8,128)(2,1)}, u32[]{:S(2)}) copy-start(bf16[16,128,641]{2,1,0:T(8,128)(2,1)} %reshape.68) | copy-start | bytes 7876612
Sparse Core Ops, SparseCore 0:
  12.0 220.8 all-gather.1
  250.4 7.2 reduce-scatter.1
where the time goes:
time: 267 us
  waiting for transfers between devices  172 us (64%)
  local copies, waits for them, and re-layouts  45.3 us (17%)
  between operations  18.8 us (7%)
  matrix products  14.3 us (5%)
  other arithmetic  12.8 us (5%)
    all_gather x1, waiting for transfers between devices, local(): lax.all_gather(templates, 'tm', axis=1, tiled=True)[0]  171 us
    reshape x4, local copies, waits for them, and re-layouts, windows(): return flattened.reshape(segment.shape[0], SPAN, seg_len + 1)[:, :, :L]  31.9 us
    dot_general x1, matrix products, local(): jnp.einsum('kcl,qcrl->kqr', lax.all_gather(templates, 'tm', axis=1, tiled...  14.3 us
    unnamed x14, local copies, waits for them, and re-layouts  8.11 us
    another operation x2, other arithmetic, slot_windows(): return jnp.stack(stacked)  6.34 us
  transfers between devices with their start and end apart: 3, of which 2 were waited for; matrix products, arithmetic and copies ran while one was open for 17% of the time, Pallas kernels for 0%

commit v1 on v0

v1 whole, which is shorter than its diff:
```python
import functools

import jax
import jax.numpy as jnp
from jax import lax
from jax.experimental import pallas as pl
from jax.experimental.pallas import tpu as pltpu
from jax.sharding import PartitionSpec as P

SPAN = 128
CODES = 32767.0
MESH = pl.DeviceIdType.MESH


def kernel(n, rows, chans, slots, span_ref, rec_ref, lhs_ref, out_ref, rec_all, shifted, hankel, acc, sib, codes, scales,
           codes_in, scales_in, e_mine, e_sib, rec_send, rec_recv, sib_send, sib_recv, code_send, code_recv,
           scale_send, scale_recv, e_send, e_recv):
    z = lax.axis_index("tm")
    core = lax.axis_index("chan")
    half = n // 2
    home = z // half
    own_part = z % half
    other = {"tm": z, "chan": 1 - core}
    blocks = n * slots

    barrier = pltpu.get_barrier_semaphore()

    def greet(i, _):
        peer = lax.rem(z + i // 2, n)
        to = lax.rem(core + i % 2, 2)
        pl.semaphore_signal(barrier, inc=1, device_id={"tm": peer, "chan": to}, device_id_type=MESH)
        return 0

    lax.fori_loop(1, 2 * n, greet, 0)
    rec_all[z] = rec_ref[...]
    rec_all[n] = jnp.zeros_like(rec_ref)
    acc[...] = jnp.zeros_like(acc)
    pl.semaphore_wait(barrier, 2 * n - 1)

    def record_copy(i):
        peer = lax.rem(z + i, n)
        return pltpu.make_async_remote_copy(
            src_ref=rec_ref, dst_ref=rec_all.at[z], send_sem=rec_send.at[peer], recv_sem=rec_recv.at[z],
            device_id={"tm": peer, "chan": core}, device_id_type=MESH)

    def record_arrival(i):
        peer = lax.rem(z + i, n)
        return pltpu.make_async_remote_copy(
            src_ref=rec_ref, dst_ref=rec_all.at[peer], send_sem=rec_send.at[peer], recv_sem=rec_recv.at[peer],
            device_id={"tm": peer, "chan": core}, device_id_type=MESH)

    lax.fori_loop(1, n, lambda i, _: (record_copy(i).start(), 0)[1], 0)
    lax.fori_loop(1, n, lambda i, _: (record_arrival(i).wait_recv(), 0)[1], 0)

    for part in range(2):
        for b in range(slots):
            piece = rec_all[z + part, :, b * SPAN:(b + 1) * SPAN].astype(jnp.float32)
            e_mine[part * slots + b:part * slots + b + 1, :] = jnp.sum(piece * piece, axis=0, keepdims=True)
    energy_copy = pltpu.make_async_remote_copy(
        src_ref=e_mine, dst_ref=e_sib, send_sem=e_send, recv_sem=e_recv, device_id=other, device_id_type=MESH)
    energy_copy.start()

    row = lax.broadcasted_iota(jnp.int32, (chans, 8, SPAN), 1)
    lane = lax.broadcasted_iota(jnp.int32, (chans, 8, SPAN), 2)

    def spread(x):
        return jnp.broadcast_to(x.astype(jnp.float32)[:, None, :], (chans, 8, SPAN))

    def shift_rows(s, _):
        for b in range(slots):
            now = spread(rec_all[s, :, b * SPAN:(b + 1) * SPAN])
            if b + 1 < slots:
                after = spread(rec_all[s, :, (b + 1) * SPAN:(b + 2) * SPAN])
            else:
                after = spread(rec_all[s + 1, :, :SPAN])
            y = jnp.where(lane >= row, now, after)
            for bit in (1, 2, 4):
                y = jnp.where((row & bit) > 0, pltpu.roll(y, SPAN - bit, 2), y)
            shifted[s * slots + b] = y
        return 0

    lax.fori_loop(0, n, shift_rows, 0)
    shifted[blocks] = jnp.zeros((chans, 8, SPAN), jnp.float32)

    def build(pair):
        for par in range(2):
            now = shifted[2 * pair + par]
            after = shifted[2 * pair + par + 1]
            for a in range(0, SPAN // 8, 2):
                both = []
                for d in (a, a + 1):
                    y = now
                    if d > 0:
                        y = pltpu.roll(jnp.where(lane >= 8 * d, now, after), SPAN - 8 * d, 2)
                    both.append(y)
                hankel[:, 8 * a:8 * a + 16, par * SPAN:(par + 1) * SPAN] = jnp.concatenate(both, axis=1).astype(jnp.bfloat16)

    def multiply(pair):
        build(pair)
        product = jnp.dot(lhs_ref[...], hankel[...].reshape(chans * SPAN, 2 * SPAN), preferred_element_type=jnp.float32)
        for par in range(2):
            for j in range(4):
                at = 2 * pair + par - j + 3
                acc[at] += product[j * rows:(j + 1) * rows, par * SPAN:(par + 1) * SPAN]

    def sibling_copy(dest):
        return pltpu.make_async_remote_copy(
            src_ref=acc.at[pl.ds(3 + slots * dest + 2 * (1 - core), 2)], dst_ref=sib.at[dest],
            send_sem=sib_send.at[dest], recv_sem=sib_recv.at[dest], device_id=other, device_id_type=MESH)

    def result_copies(dest, part, from_core):
        to = {"tm": dest, "chan": home}
        slot = part * 2 + from_core
        return (
            pltpu.make_async_remote_copy(
                src_ref=codes.at[dest], dst_ref=codes_in.at[part, pl.ds(2 * from_core, 2)], send_sem=code_send.at[dest],
                recv_sem=code_recv.at[slot], device_id=to, device_id_type=MESH),
            pltpu.make_async_remote_copy(
                src_ref=scales.at[dest], dst_ref=scales_in.at[part, pl.ds(2 * from_core, 2)], send_sem=scale_send.at[dest],
                recv_sem=scale_recv.at[slot], device_id=to, device_id_type=MESH),
        )

    def finish(dest):
        sibling_copy(dest).wait_recv()
        keep = jnp.logical_and(dest == z, core == home)
        for b in range(2):
            total = acc[3 + slots * dest + 2 * core + b] + sib[dest, b]
            top = jnp.maximum(jnp.max(jnp.abs(total), axis=0, keepdims=True), 1e-37)
            coded = jnp.round((total * (1.0 / top)) * CODES).astype(jnp.int32).astype(jnp.int16)
            scale = jnp.broadcast_to(top * (1.0 / CODES), (8, SPAN))

            @pl.when(keep)
            def _():
                codes_in[own_part, 2 * core + b] = coded
                scales_in[own_part, 2 * core + b] = scale

            @pl.when(jnp.logical_not(keep))
            def _():
                codes[dest, b] = coded
                scales[dest, b] = scale

        @pl.when(jnp.logical_not(keep))
        def _():
            for copy in result_copies(dest, own_part, core):
                copy.start()

    def step(d, _):
        dest = n - 1 - d
        multiply(2 * dest + 1)
        multiply(2 * dest)
        sibling_copy(dest).start()

        @pl.when(d > 0)
        def _():
            finish(dest + 1)

        return 0

    lax.fori_loop(0, n, step, 0)
    finish(0)

    energy_copy.wait()
    e = e_mine[...] + e_sib[...]
    i0 = lax.broadcasted_iota(jnp.int32, (SPAN, SPAN), 0)
    i1 = lax.broadcasted_iota(jnp.int32, (SPAN, SPAN), 1)
    dot = functools.partial(jnp.dot, preferred_element_type=jnp.float32, precision=lax.Precision.HIGHEST)
    tails = dot(e, jnp.where(i0 >= i1, 1.0, 0.0))
    heads = dot(e, jnp.where(i0 < i1, 1.0, 0.0))
    sums = jnp.sum(e, axis=1, keepdims=True)
    for b in range(slots):
        energy = tails[b:b + 1] + heads[b + 4:b + 5] + sums[b + 1:b + 2] + sums[b + 2:b + 3] + sums[b + 3:b + 4]
        e_mine[b:b + 1, :] = lax.rsqrt(energy / (2 * chans * 4 * SPAN) + 1e-05)

    def arrival(i, _):
        part, from_core = i // 2, i % 2
        source = core * half + part

        @pl.when(jnp.logical_not(jnp.logical_and(source == z, from_core == core)))
        def _():
            for copy in result_copies(0, part, from_core):
                copy.wait_recv()

        return 0

    lax.fori_loop(0, n, arrival, 0)

    for slot in range(slots):
        at = span_ref[0, slot]
        block = jnp.maximum(at, 0)
        inverse = jnp.where(at >= 0, e_mine[pl.ds(block, 1), :], 0.0)
        for part in range(half):
            values = codes_in[part, block].astype(jnp.int32).astype(jnp.float32)
            scale = scales_in[part, block, 0:1] * inverse
            out_ref[part * rows:(part + 1) * rows, slot * SPAN:(slot + 1) * SPAN] = values * scale

    def drain(dest, _):
        sibling_copy(dest).wait_send()

        @pl.when(jnp.logical_not(jnp.logical_and(dest == z, core == home)))
        def _():
            for copy in result_copies(dest, own_part, core):
                copy.wait_send()

        @pl.when(dest != z)
        def _():
            pltpu.make_async_remote_copy(
                src_ref=rec_ref, dst_ref=rec_all.at[z], send_sem=rec_send.at[dest], recv_sem=rec_recv.at[z],
                device_id={"tm": dest, "chan": core}, device_id_type=MESH).wait_send()

        return 0

    lax.fori_loop(0, n, drain, 0)


def local(n, record, templates, span_list):
    _, rows, chans, length = templates.shape
    slots = span_list.shape[1]
    blocks = n * slots
    lhs = templates[0].reshape(rows, chans, length // SPAN, SPAN).transpose(2, 0, 1, 3).reshape(4 * rows, chans * SPAN)
    vmem = pl.BlockSpec(memory_space=pltpu.VMEM)
    dma = pltpu.SemaphoreType.DMA
    return pl.pallas_call(
        functools.partial(kernel, n, rows, chans, slots),
        out_shape=jax.ShapeDtypeStruct((rows * n // 2, slots * SPAN), jnp.float32),
        in_specs=[pl.BlockSpec(memory_space=pltpu.SMEM), vmem, vmem],
        out_specs=vmem,
        scratch_shapes=[
            pltpu.VMEM((n + 1, chans, record.shape[1]), jnp.bfloat16),
            pltpu.VMEM((blocks + 1, chans, 8, SPAN), jnp.float32),
            pltpu.VMEM((chans, SPAN, 2 * SPAN), jnp.bfloat16),
            pltpu.VMEM((blocks + 3, rows, SPAN), jnp.float32),
            pltpu.VMEM((n, 2, rows, SPAN), jnp.float32),
            pltpu.VMEM((n, 2, rows, SPAN), jnp.int16),
            pltpu.VMEM((n, 2, 8, SPAN), jnp.float32),
            pltpu.VMEM((n // 2, 4, rows, SPAN), jnp.int16),
            pltpu.VMEM((n // 2, 4, 8, SPAN), jnp.float32),
            pltpu.VMEM((8, SPAN), jnp.float32),
            pltpu.VMEM((8, SPAN), jnp.float32),
            dma((n,)), dma((n,)), dma((n,)), dma((n,)), dma((n,)), dma((n,)), dma((n,)), dma((n,)),
            dma, dma,
        ],
        compiler_params=pltpu.CompilerParams(collective_id=0, has_side_effects=True, vmem_limit_bytes=50 * 2**20),
    )(span_list, record, lhs)


def solution(mesh):
    in_specs = (P("chan", ("grp", "tm")), P("tmpl", "tm", "chan", None), P(("grp", "tm"), None))
    out_specs = P(("tmpl", "chan"), ("grp", "tm"))
    return jax.shard_map(functools.partial(local, mesh.shape["tm"]), mesh=mesh, in_specs=in_specs, out_specs=out_specs, check_vma=False)
```

time: 267 us -> 36.5 us (0.14)
  the two profiles are of different devices: /device:TPU:0 before, /device:TPU:1 now
where the time goes in v1:
time: 36.5 us; the launch traced here: 36.4 us
  Pallas kernels  29.9 us (82%)
  local copies, waits for them, and re-layouts  6.37 us (17%)
    pallas_call x1, Pallas kernels, local(): pl.pallas_call(functools.partial(kernel, n, rows, chans, slots), out_shap...  29.9 us
    another operation x2, local copies, waits for them, and re-layouts, local(): templates[0].reshape(rows, chans, length // SPAN, SPAN)  4.16 us
    unnamed x6, local copies, waits for them, and re-layouts  2.2 us

profile of v1, /device:TPU:1, one launch (start us, length us, event | category | flops | bytes accessed | tf_op | source)
XLA Modules:
  0.0 36.4 jit_solution(11038285888669545914)
XLA Ops:
  0.0 3.8 %reshape_squeeze.3 = bf16[192,16,4,128]{3,2,1,0:T(4,128)(2,1)S(1)} reshape(bf16[1,192,16,512]{3,2,1,0:T(8,128)(2,1)} %param.4) | data formatting | bytes 6291456 | tf_op jit(solution)/shard_map/reshape;squeeze | solution.py:219
  3.8 0.4 %copy.4 = bf16[192,16,4,128]{3,1,0,2:T(8,128)(2,1)S(1)} copy(bf16[192,16,4,128]{3,2,1,0:T(4,128)(2,1)S(1)} %reshape_squeeze.3) | data formatting | bytes 6291456 | tf_op jit(solution)/shard_map/reshape;squeeze | solution.py:219
  4.2 0.0 copy-start
  4.2 0.0 copy-start.1
  4.2 1.3 %copy.7 = bf16[96,8,16,128]{3,1,2,0:T(8,128)(2,1)S(1)} copy(bf16[96,8,16,128]{3,2,1,0:T(8,128)(2,1)S(1)} %bitcast.9) | data formatting | bytes 6291456
  5.5 0.0 copy-done
  5.5 0.0 copy-done.1
  5.5 29.9 %shard_map.37 = f32[384,512]{1,0:T(8,128)S(1)} custom-call(s32[1,4]{1,0:T(1,128)S(1)} %copy-done.1, bf16[16,512]{1,0:T(8,128)(2,1)S(1)} %copy-done, bf16[768,2048]{1,0:T(8,128)(2,1)S(1)} %bitcast.8), custom_call_target="tpu_custom_call" | custom-call | tf_op jit(solution)/shard_map/pallas_call | solution.py:222
  35.5 0.9 %copy.9 = f32[384,512]{1,0:T(8,128)} copy(f32[384,512]{1,0:T(8,128)S(1)} %shard_map.37) | data formatting | bytes 1572864
Async XLA Ops:
  4.2 1.3 %copy-start = (bf16[16,512]{1,0:T(8,128)(2,1)S(1)}, bf16[16,512]{1,0:T(8,128)(2,1)}, u32[]{:S(2)}) copy-start(bf16[16,512]{1,0:T(8,128)(2,1)} %rec_ref.1) | copy-start | bytes 49156
  4.2 1.3 %copy-start.1 = (s32[1,4]{1,0:T(1,128)S(1)}, s32[1,4]{1,0:T(1,128)}, u32[]{:S(2)}) copy-start(s32[1,4]{1,0:T(1,128)} %span_ref.1) | copy-start | bytes 52

commit v2 on v1

--- a/solution.py
+++ b/solution.py
@@ -12,9 +12,9 @@
 MESH = pl.DeviceIdType.MESH
 
 
-def kernel(n, rows, chans, slots, span_ref, rec_ref, lhs_ref, out_ref, rec_all, shifted, hankel, acc, sib, codes, scales,
+def kernel(n, rows, chans, slots, span_ref, rec_ref, tmpl_ref, out_ref, tmpl, lhs, rec_all, shifted, hankel_a, hankel_b, acc, sib, codes, scales,
            codes_in, scales_in, e_mine, e_sib, rec_send, rec_recv, sib_send, sib_recv, code_send, code_recv,
-           scale_send, scale_recv, e_send, e_recv):
+           scale_send, scale_recv, e_send, e_recv, tmpl_sem):
     z = lax.axis_index("tm")
     core = lax.axis_index("chan")
     half = n // 2
@@ -23,6 +23,8 @@
     other = {"tm": z, "chan": 1 - core}
     blocks = n * slots
 
+    tmpl_copy = pltpu.make_async_copy(tmpl_ref.at[0], tmpl, tmpl_sem)
+    tmpl_copy.start()
     barrier = pltpu.get_barrier_semaphore()
 
     def greet(i, _):
@@ -50,6 +52,19 @@
             device_id={"tm": peer, "chan": core}, device_id_type=MESH)
 
     lax.fori_loop(1, n, lambda i, _: (record_copy(i).start(), 0)[1], 0)
+
+    tmpl_copy.wait()
+    group = 16 if rows % 16 == 0 else 8
+
+    def arrange(g, _):
+        for j in range(4):
+            turned = jnp.swapaxes(tmpl[pl.ds(g * group, group), :, j * SPAN:(j + 1) * SPAN], 0, 1)
+            at = pl.multiple_of(j * rows + g * group, group)
+            for c in range(chans):
+                lhs[pl.ds(at, group), c * SPAN:(c + 1) * SPAN] = turned[c]
+        return 0
+
+    lax.fori_loop(0, rows // group, arrange, 0)
     lax.fori_loop(1, n, lambda i, _: (record_arrival(i).wait_recv(), 0)[1], 0)
 
     for part in range(2):
@@ -82,7 +97,7 @@
     lax.fori_loop(0, n, shift_rows, 0)
     shifted[blocks] = jnp.zeros((chans, 8, SPAN), jnp.float32)
 
-    def build(pair):
+    def build(pair, hankel):
         for par in range(2):
             now = shifted[2 * pair + par]
             after = shifted[2 * pair + par + 1]
@@ -95,69 +110,89 @@
                     both.append(y)
                 hankel[:, 8 * a:8 * a + 16, par * SPAN:(par + 1) * SPAN] = jnp.concatenate(both, axis=1).astype(jnp.bfloat16)
 
-    def multiply(pair):
-        build(pair)
-        product = jnp.dot(lhs_ref[...], hankel[...].reshape(chans * SPAN, 2 * SPAN), preferred_element_type=jnp.float32)
+    def multiply(pair, hankel):
+        product = jnp.dot(lhs[...], hankel[...].reshape(chans * SPAN, 2 * SPAN), preferred_element_type=jnp.float32)
         for par in range(2):
             for j in range(4):
                 at = 2 * pair + par - j + 3
                 acc[at] += product[j * rows:(j + 1) * rows, par * SPAN:(par + 1) * SPAN]
 
-    def sibling_copy(dest):
+    rising = jnp.where(z >= half, 1, 0)
+
+    def pair_at(t):
+        return rising * t + (1 - rising) * (2 * n - 1 - t)
+
+    def chunk_at(t):
+        return pair_at(t) - 2 * rising
+
+    def sibling_copy(u):
         return pltpu.make_async_remote_copy(
-            src_ref=acc.at[pl.ds(3 + slots * dest + 2 * (1 - core), 2)], dst_ref=sib.at[dest],
-            send_sem=sib_send.at[dest], recv_sem=sib_recv.at[dest], device_id=other, device_id_type=MESH)
-
-    def result_copies(dest, part, from_core):
-        to = {"tm": dest, "chan": home}
-        slot = part * 2 + from_core
+            src_ref=acc.at[pl.ds(3 + 2 * u, 2)], dst_ref=sib.at[u],
+            send_sem=sib_send.at[u], recv_sem=sib_recv.at[u], device_id=other, device_id_type=MESH)
+
+    def result_copies(u, part):
+        to = {"tm": u // 2, "chan": home}
+        slot = part * 2 + u % 2
         return (
             pltpu.make_async_remote_copy(
-                src_ref=codes.at[dest], dst_ref=codes_in.at[part, pl.ds(2 * from_core, 2)], send_sem=code_send.at[dest],
+                src_ref=codes.at[u], dst_ref=codes_in.at[part, pl.ds(2 * (u % 2), 2)], send_sem=code_send.at[u],
                 recv_sem=code_recv.at[slot], device_id=to, device_id_type=MESH),
             pltpu.make_async_remote_copy(
-                src_ref=scales.at[dest], dst_ref=scales_in.at[part, pl.ds(2 * from_core, 2)], send_sem=scale_send.at[dest],
+                src_ref=scales.at[u], dst_ref=scales_in.at[part, pl.ds(2 * (u % 2), 2)], send_sem=scale_send.at[u],
                 recv_sem=scale_recv.at[slot], device_id=to, device_id_type=MESH),
         )
 
-    def finish(dest):
-        sibling_copy(dest).wait_recv()
-        keep = jnp.logical_and(dest == z, core == home)
-        for b in range(2):
-            total = acc[3 + slots * dest + 2 * core + b] + sib[dest, b]
-            top = jnp.maximum(jnp.max(jnp.abs(total), axis=0, keepdims=True), 1e-37)
-            coded = jnp.round((total * (1.0 / top)) * CODES).astype(jnp.int32).astype(jnp.int16)
-            scale = jnp.broadcast_to(top * (1.0 / CODES), (8, SPAN))
-
-            @pl.when(keep)
-            def _():
-                codes_in[own_part, 2 * core + b] = coded
-                scales_in[own_part, 2 * core + b] = scale
+    def hand_over(u):
+        @pl.when(jnp.logical_and(jnp.logical_and(u >= 0, u < 2 * n), lax.rem(u + 2, 2) != core))
+        def _():
+            sibling_copy(u).start()
+
+    def finish(u):
+        @pl.when(jnp.logical_and(jnp.logical_and(u >= 0, u < 2 * n), lax.rem(u + 2, 2) == core))
+        def _():
+            sibling_copy(u).wait_recv()
+            keep = jnp.logical_and(u // 2 == z, core == home)
+            for b in range(2):
+                total = acc[3 + 2 * u + b] + sib[u, b]
+                top = jnp.maximum(jnp.max(jnp.abs(total), axis=0, keepdims=True), 1e-37)
+                coded = jnp.round((total * (1.0 / top)) * CODES).astype(jnp.int32).astype(jnp.int16)
+                scale = jnp.broadcast_to(top * (1.0 / CODES), (8, SPAN))
+
+                @pl.when(keep)
+                def _():
+                    codes_in[own_part, 2 * core + b] = coded
+                    scales_in[own_part, 2 * core + b] = scale
+
+                @pl.when(jnp.logical_not(keep))
+                def _():
+                    codes[u, b] = coded
+                    scales[u, b] = scale
 
             @pl.when(jnp.logical_not(keep))
             def _():
-                codes[dest, b] = coded
-                scales[dest, b] = scale
-
-        @pl.when(jnp.logical_not(keep))
-        def _():
-            for copy in result_copies(dest, own_part, core):
-                copy.start()
-
-    def step(d, _):
-        dest = n - 1 - d
-        multiply(2 * dest + 1)
-        multiply(2 * dest)
-        sibling_copy(dest).start()
-
-        @pl.when(d > 0)
-        def _():
-            finish(dest + 1)
-
+                for copy in result_copies(u, own_part):
+                    copy.start()
+
+    build(pair_at(0), hankel_a)
+
+    def step(i, _):
+        t = 2 * i
+        build(pair_at(t + 1), hankel_b)
+        multiply(pair_at(t), hankel_a)
+        hand_over(chunk_at(t))
+        finish(chunk_at(t - 1))
+        build(jnp.clip(pair_at(t + 2), 0, 2 * n - 1), hankel_a)
+        multiply(pair_at(t + 1), hankel_b)
+        hand_over(chunk_at(t + 1))
+        finish(chunk_at(t))
         return 0
 
     lax.fori_loop(0, n, step, 0)
-    finish(0)
+    hand_over(chunk_at(2 * n))
+    hand_over(chunk_at(2 * n + 1))
+    finish(chunk_at(2 * n - 1))
+    finish(chunk_at(2 * n))
+    finish(chunk_at(2 * n + 1))
 
     energy_copy.wait()
     e = e_mine[...] + e_sib[...]
@@ -177,7 +212,7 @@
 
         @pl.when(jnp.logical_not(jnp.logical_and(source == z, from_core == core)))
         def _():
-            for copy in result_copies(0, part, from_core):
+            for copy in result_copies(from_core, part):
                 copy.wait_recv()
 
         return 0
@@ -193,54 +228,55 @@
             scale = scales_in[part, block, 0:1] * inverse
             out_ref[part * rows:(part + 1) * rows, slot * SPAN:(slot + 1) * SPAN] = values * scale
 
-    def drain(dest, _):
-        sibling_copy(dest).wait_send()
-
-        @pl.when(jnp.logical_not(jnp.logical_and(dest == z, core == home)))
-        def _():
-            for copy in result_copies(dest, own_part, core):
+    def drain(u, _):
+        mine = u % 2 == core
+
+        @pl.when(jnp.logical_not(mine))
+        def _():
+            sibling_copy(u).wait_send()
+
+        @pl.when(jnp.logical_and(mine, jnp.logical_not(jnp.logical_and(u // 2 == z, core == home))))
+        def _():
+            for copy in result_copies(u, own_part):
                 copy.wait_send()
 
-        @pl.when(dest != z)
-        def _():
-            pltpu.make_async_remote_copy(
-                src_ref=rec_ref, dst_ref=rec_all.at[z], send_sem=rec_send.at[dest], recv_sem=rec_recv.at[z],
-                device_id={"tm": dest, "chan": core}, device_id_type=MESH).wait_send()
-
-        return 0
-
-    lax.fori_loop(0, n, drain, 0)
+        return 0
+
+    lax.fori_loop(0, 2 * n, drain, 0)
+    lax.fori_loop(1, n, lambda i, _: (record_copy(i).wait_send(), 0)[1], 0)
 
 
 def local(n, record, templates, span_list):
-    _, rows, chans, length = templates.shape
+    _, rows, chans, _ = templates.shape
     slots = span_list.shape[1]
     blocks = n * slots
-    lhs = templates[0].reshape(rows, chans, length // SPAN, SPAN).transpose(2, 0, 1, 3).reshape(4 * rows, chans * SPAN)
     vmem = pl.BlockSpec(memory_space=pltpu.VMEM)
     dma = pltpu.SemaphoreType.DMA
     return pl.pallas_call(
         functools.partial(kernel, n, rows, chans, slots),
         out_shape=jax.ShapeDtypeStruct((rows * n // 2, slots * SPAN), jnp.float32),
-        in_specs=[pl.BlockSpec(memory_space=pltpu.SMEM), vmem, vmem],
+        in_specs=[pl.BlockSpec(memory_space=pltpu.SMEM), vmem, pl.BlockSpec(memory_space=pltpu.HBM)],
         out_specs=vmem,
         scratch_shapes=[
+            pltpu.VMEM(templates.shape[1:], jnp.bfloat16),
+            pltpu.VMEM((4 * rows, chans * SPAN), jnp.bfloat16),
             pltpu.VMEM((n + 1, chans, record.shape[1]), jnp.bfloat16),
             pltpu.VMEM((blocks + 1, chans, 8, SPAN), jnp.float32),
             pltpu.VMEM((chans, SPAN, 2 * SPAN), jnp.bfloat16),
+            pltpu.VMEM((chans, SPAN, 2 * SPAN), jnp.bfloat16),
             pltpu.VMEM((blocks + 3, rows, SPAN), jnp.float32),
-            pltpu.VMEM((n, 2, rows, SPAN), jnp.float32),
-            pltpu.VMEM((n, 2, rows, SPAN), jnp.int16),
-            pltpu.VMEM((n, 2, 8, SPAN), jnp.float32),
+            pltpu.VMEM((2 * n, 2, rows, SPAN), jnp.float32),
+            pltpu.VMEM((2 * n, 2, rows, SPAN), jnp.int16),
+            pltpu.VMEM((2 * n, 2, 8, SPAN), jnp.float32),
             pltpu.VMEM((n // 2, 4, rows, SPAN), jnp.int16),
             pltpu.VMEM((n // 2, 4, 8, SPAN), jnp.float32),
             pltpu.VMEM((8, SPAN), jnp.float32),
             pltpu.VMEM((8, SPAN), jnp.float32),
-            dma((n,)), dma((n,)), dma((n,)), dma((n,)), dma((n,)), dma((n,)), dma((n,)), dma((n,)),
-            dma, dma,
+            dma((n,)), dma((n,)), dma((2 * n,)), dma((2 * n,)), dma((2 * n,)), dma((n,)), dma((2 * n,)), dma((n,)),
+            dma, dma, dma,
         ],
-        compiler_params=pltpu.CompilerParams(collective_id=0, has_side_effects=True, vmem_limit_bytes=50 * 2**20),
-    )(span_list, record, lhs)
+        compiler_params=pltpu.CompilerParams(collective_id=0, has_side_effects=True, vmem_limit_bytes=62 * 2**20),
+    )(span_list, record, templates)
 
 
 def solution(mesh):

time: 36.5 us -> 33.7 us (0.923)
  the two profiles are of different devices: /device:TPU:1 before, /device:TPU:0 now
where the time goes in v2:
time: 33.7 us; the launch traced here: 33.5 us
  Pallas kernels  31.4 us (93%)
  local copies, waits for them, and re-layouts  2.06 us (6%)
    pallas_call x1, Pallas kernels, local(): pl.pallas_call(functools.partial(kernel, n, rows, chans, slots), out_shap...  31.4 us
    unnamed x1, local copies, waits for them, and re-layouts  2.06 us

profile of v2, /device:TPU:0, one launch (start us, length us, event | category | flops | bytes accessed | tf_op | source)
XLA Modules:
  0.0 33.5 jit_solution(12310562003531908846)
XLA Ops:
  0.0 31.4 %shard_map.37 = f32[384,512]{1,0:T(8,128)} custom-call(s32[1,4]{1,0:T(1,128)} %span_ref.1, bf16[16,512]{1,0:T(8,128)(2,1)} %rec_ref.1, bf16[1,192,16,512]{3,2,1,0:T(8,128)(2,1)} %tmpl_ref.1), custom_call_target="tpu_custom_call" | custom-call | tf_op jit(solution)/shard_map/pallas_call | solution.py:255
  31.4 2.1 %copy.5 = f32[384,512]{1,0:T(8,128)} copy(f32[384,512]{1,0:T(8,128)} %shard_map.37) | data formatting | bytes 1572864

commit v3 on v2

--- a/solution.py
+++ b/solution.py
@@ -12,7 +12,7 @@
 MESH = pl.DeviceIdType.MESH
 
 
-def kernel(n, rows, chans, slots, span_ref, rec_ref, tmpl_ref, out_ref, tmpl, lhs, rec_all, shifted, hankel_a, hankel_b, acc, sib, codes, scales,
+def kernel(n, rows, chans, slots, span_ref, rec_ref, tmpl_ref, out_ref, tmpl, lhs, rec_all, ring_a, ring_b, ring_c, ring_d, acc, sib, codes, scales,
            codes_in, scales_in, e_mine, e_sib, rec_send, rec_recv, sib_send, sib_recv, code_send, code_recv,
            scale_send, scale_recv, e_send, e_recv, tmpl_sem):
     z = lax.axis_index("tm")
@@ -21,7 +21,7 @@
     home = z // half
     own_part = z % half
     other = {"tm": z, "chan": 1 - core}
-    blocks = n * slots
+    ring = (ring_a, ring_b, ring_c, ring_d)
 
     tmpl_copy = pltpu.make_async_copy(tmpl_ref.at[0], tmpl, tmpl_sem)
     tmpl_copy.start()
@@ -36,23 +36,7 @@
     lax.fori_loop(1, 2 * n, greet, 0)
     rec_all[z] = rec_ref[...]
     rec_all[n] = jnp.zeros_like(rec_ref)
-    acc[...] = jnp.zeros_like(acc)
-    pl.semaphore_wait(barrier, 2 * n - 1)
-
-    def record_copy(i):
-        peer = lax.rem(z + i, n)
-        return pltpu.make_async_remote_copy(
-            src_ref=rec_ref, dst_ref=rec_all.at[z], send_sem=rec_send.at[peer], recv_sem=rec_recv.at[z],
-            device_id={"tm": peer, "chan": core}, device_id_type=MESH)
-
-    def record_arrival(i):
-        peer = lax.rem(z + i, n)
-        return pltpu.make_async_remote_copy(
-            src_ref=rec_ref, dst_ref=rec_all.at[peer], send_sem=rec_send.at[peer], recv_sem=rec_recv.at[peer],
-            device_id={"tm": peer, "chan": core}, device_id_type=MESH)
-
-    lax.fori_loop(1, n, lambda i, _: (record_copy(i).start(), 0)[1], 0)
-
+    rec_all[n + 1] = jnp.zeros_like(rec_ref)
     tmpl_copy.wait()
     group = 16 if rows % 16 == 0 else 8
 
@@ -63,6 +47,22 @@
             for c in range(chans):
                 lhs[pl.ds(at, group), c * SPAN:(c + 1) * SPAN] = turned[c]
         return 0
+
+    pl.semaphore_wait(barrier, 2 * n - 1)
+
+    def record_copy(i):
+        peer = lax.rem(z + i, n)
+        return pltpu.make_async_remote_copy(
+            src_ref=rec_ref, dst_ref=rec_all.at[z], send_sem=rec_send.at[peer], recv_sem=rec_recv.at[z],
+            device_id={"tm": peer, "chan": core}, device_id_type=MESH)
+
+    def record_arrival(i):
+        peer = lax.rem(z + i, n)
+        return pltpu.make_async_remote_copy(
+            src_ref=rec_ref, dst_ref=rec_all.at[peer], send_sem=rec_send.at[peer], recv_sem=rec_recv.at[peer],
+            device_id={"tm": peer, "chan": core}, device_id_type=MESH)
+
+    lax.fori_loop(1, n, lambda i, _: (record_copy(i).start(), 0)[1], 0)
 
     lax.fori_loop(0, rows // group, arrange, 0)
     lax.fori_loop(1, n, lambda i, _: (record_arrival(i).wait_recv(), 0)[1], 0)
@@ -81,26 +81,21 @@
     def spread(x):
         return jnp.broadcast_to(x.astype(jnp.float32)[:, None, :], (chans, 8, SPAN))
 
-    def shift_rows(s, _):
-        for b in range(slots):
-            now = spread(rec_all[s, :, b * SPAN:(b + 1) * SPAN])
-            if b + 1 < slots:
-                after = spread(rec_all[s, :, (b + 1) * SPAN:(b + 2) * SPAN])
-            else:
-                after = spread(rec_all[s + 1, :, :SPAN])
-            y = jnp.where(lane >= row, now, after)
-            for bit in (1, 2, 4):
-                y = jnp.where((row & bit) > 0, pltpu.roll(y, SPAN - bit, 2), y)
-            shifted[s * slots + b] = y
-        return 0
-
-    lax.fori_loop(0, n, shift_rows, 0)
-    shifted[blocks] = jnp.zeros((chans, 8, SPAN), jnp.float32)
+    def block_at(at):
+        lanes = pl.multiple_of(lax.rem(at, slots) * SPAN, SPAN)
+        return spread(rec_all[at // slots, :, pl.ds(lanes, SPAN)])
+
+    def shift_rows(now, after):
+        y = jnp.where(lane >= row, now, after)
+        for bit in (1, 2, 4):
+            y = jnp.where((row & bit) > 0, pltpu.roll(y, SPAN - bit, 2), y)
+        return y
 
     def build(pair, hankel):
+        raw = [block_at(2 * pair + i) for i in (0, 1, 2, 2)]
+        shifted = [shift_rows(raw[i], raw[i + 1]) for i in range(3)]
         for par in range(2):
-            now = shifted[2 * pair + par]
-            after = shifted[2 * pair + par + 1]
+            now, after = shifted[par], shifted[par + 1]
             for a in range(0, SPAN // 8, 2):
                 both = []
                 for d in (a, a + 1):
@@ -110,24 +105,36 @@
                     both.append(y)
                 hankel[:, 8 * a:8 * a + 16, par * SPAN:(par + 1) * SPAN] = jnp.concatenate(both, axis=1).astype(jnp.bfloat16)
 
-    def multiply(pair, hankel):
-        product = jnp.dot(lhs[...], hankel[...].reshape(chans * SPAN, 2 * SPAN), preferred_element_type=jnp.float32)
+    def multiply(u, first, second, third):
+        depth = chans * SPAN
+
+        def straddle(left, right):
+            return jnp.concatenate([left[:, :, SPAN:].reshape(depth, SPAN), right[:, :, :SPAN].reshape(depth, SPAN)], axis=1)
+
+        sides = (first[...].reshape(depth, 2 * SPAN), straddle(first, second),
+                 second[...].reshape(depth, 2 * SPAN), straddle(second, third))
+        product = None
+        for j in range(4):
+            term = jnp.dot(lhs[j * rows:(j + 1) * rows, :], sides[j], preferred_element_type=jnp.float32)
+            product = term if product is None else product + term
         for par in range(2):
-            for j in range(4):
-                at = 2 * pair + par - j + 3
-                acc[at] += product[j * rows:(j + 1) * rows, par * SPAN:(par + 1) * SPAN]
-
-    rising = jnp.where(z >= half, 1, 0)
+            acc[2 * u + par] = product[:, par * SPAN:(par + 1) * SPAN]
+
+    upper = jnp.where(z >= half, 1, 0)
+    turn = (1 - upper) * (2 * n + 2) + upper * (n + 2)
 
     def pair_at(t):
-        return rising * t + (1 - rising) * (2 * n - 1 - t)
+        wrapped = jnp.where(t >= turn, 1, 0)
+        return (1 - wrapped) * (turn - 1 - t) + wrapped * jnp.maximum(2 * n + 1 - (t - turn), 0)
 
     def chunk_at(t):
-        return pair_at(t) - 2 * rising
+        wrapped = jnp.where(t >= turn, 1, 0)
+        use = jnp.logical_and(t - wrapped * turn >= 2, jnp.logical_and(t >= 0, t < 2 * n + 2 + 2 * upper))
+        return jnp.where(use, pair_at(t), -1)
 
     def sibling_copy(u):
         return pltpu.make_async_remote_copy(
-            src_ref=acc.at[pl.ds(3 + 2 * u, 2)], dst_ref=sib.at[u],
+            src_ref=acc.at[pl.ds(2 * u, 2)], dst_ref=sib.at[u],
             send_sem=sib_send.at[u], recv_sem=sib_recv.at[u], device_id=other, device_id_type=MESH)
 
     def result_copies(u, part):
@@ -153,7 +160,7 @@
             sibling_copy(u).wait_recv()
             keep = jnp.logical_and(u // 2 == z, core == home)
             for b in range(2):
-                total = acc[3 + 2 * u + b] + sib[u, b]
+                total = acc[2 * u + b] + sib[u, b]
                 top = jnp.maximum(jnp.max(jnp.abs(total), axis=0, keepdims=True), 1e-37)
                 coded = jnp.round((total * (1.0 / top)) * CODES).astype(jnp.int32).astype(jnp.int16)
                 scale = jnp.broadcast_to(top * (1.0 / CODES), (8, SPAN))
@@ -173,26 +180,29 @@
                 for copy in result_copies(u, own_part):
                     copy.start()
 
-    build(pair_at(0), hankel_a)
+    build(pair_at(0), ring[0])
 
     def step(i, _):
-        t = 2 * i
-        build(pair_at(t + 1), hankel_b)
-        multiply(pair_at(t), hankel_a)
-        hand_over(chunk_at(t))
-        finish(chunk_at(t - 1))
-        build(jnp.clip(pair_at(t + 2), 0, 2 * n - 1), hankel_a)
-        multiply(pair_at(t + 1), hankel_b)
-        hand_over(chunk_at(t + 1))
-        finish(chunk_at(t))
-        return 0
-
-    lax.fori_loop(0, n, step, 0)
-    hand_over(chunk_at(2 * n))
-    hand_over(chunk_at(2 * n + 1))
-    finish(chunk_at(2 * n - 1))
-    finish(chunk_at(2 * n))
-    finish(chunk_at(2 * n + 1))
+        for r in range(4):
+            t = 4 * i + r
+            u = chunk_at(t)
+            following = pair_at(jnp.minimum(t + 1, 2 * n + 3))
+
+            @pl.when(u >= 0)
+            def _():
+                build(following, ring[(r + 1) % 4])
+                multiply(u, ring[r], ring[(r + 3) % 4], ring[(r + 2) % 4])
+
+            @pl.when(jnp.logical_and(u < 0, t + 1 < 2 * n + 2 + 2 * upper))
+            def _():
+                build(following, ring[(r + 1) % 4])
+
+            hand_over(u)
+            finish(chunk_at(t - 1))
+        return 0
+
+    lax.fori_loop(0, (2 * n + 4) // 4, step, 0)
+    finish(chunk_at(2 * n + 3))
 
     energy_copy.wait()
     e = e_mine[...] + e_sib[...]
@@ -249,7 +259,6 @@
 def local(n, record, templates, span_list):
     _, rows, chans, _ = templates.shape
     slots = span_list.shape[1]
-    blocks = n * slots
     vmem = pl.BlockSpec(memory_space=pltpu.VMEM)
     dma = pltpu.SemaphoreType.DMA
     return pl.pallas_call(
@@ -260,11 +269,12 @@
         scratch_shapes=[
             pltpu.VMEM(templates.shape[1:], jnp.bfloat16),
             pltpu.VMEM((4 * rows, chans * SPAN), jnp.bfloat16),
-            pltpu.VMEM((n + 1, chans, record.shape[1]), jnp.bfloat16),
-            pltpu.VMEM((blocks + 1, chans, 8, SPAN), jnp.float32),
-            pltpu.VMEM((chans, SPAN, 2 * SPAN), jnp.bfloat16),
-            pltpu.VMEM((chans, SPAN, 2 * SPAN), jnp.bfloat16),
-            pltpu.VMEM((blocks + 3, rows, SPAN), jnp.float32),
+            pltpu.VMEM((n + 2, chans, record.shape[1]), jnp.bfloat16),
+            pltpu.VMEM((chans, SPAN, 2 * SPAN), jnp.bfloat16),
+            pltpu.VMEM((chans, SPAN, 2 * SPAN), jnp.bfloat16),
+            pltpu.VMEM((chans, SPAN, 2 * SPAN), jnp.bfloat16),
+            pltpu.VMEM((chans, SPAN, 2 * SPAN), jnp.bfloat16),
+            pltpu.VMEM((4 * n, rows, SPAN), jnp.float32),
             pltpu.VMEM((2 * n, 2, rows, SPAN), jnp.float32),
             pltpu.VMEM((2 * n, 2, rows, SPAN), jnp.int16),
             pltpu.VMEM((2 * n, 2, 8, SPAN), jnp.float32),

time: 33.7 us -> 30.7 us (0.911)
  Pallas kernels: 31.4 us -> 28.4 us
    pallas_call x1, Pallas kernels: 31.4 us -> 28.4 us  [local(): pl.pallas_call(functools.partial(kernel, n, rows, chans, slots), out_shap...]
where the time goes in v3:
time: 30.7 us; the launch traced here: 30.4 us
  Pallas kernels  28.4 us (93%)
  local copies, waits for them, and re-layouts  2.06 us (7%)
    pallas_call x1, Pallas kernels, local(): pl.pallas_call(functools.partial(kernel, n, rows, chans, slots), out_shap...  28.4 us
    unnamed x1, local copies, waits for them, and re-layouts  2.06 us

profile of v3, /device:TPU:0, one launch (start us, length us, event | category | flops | bytes accessed | tf_op | source)
XLA Modules:
  0.0 30.4 jit_solution(3354315848546198429)
XLA Ops:
  0.0 28.4 %shard_map.37 = f32[384,512]{1,0:T(8,128)} custom-call(s32[1,4]{1,0:T(1,128)} %span_ref.1, bf16[16,512]{1,0:T(8,128)(2,1)} %rec_ref.1, bf16[1,192,16,512]{3,2,1,0:T(8,128)(2,1)} %tmpl_ref.1), custom_call_target="tpu_custom_call" | custom-call | tf_op jit(solution)/shard_map/pallas_call | solution.py:264
  28.4 2.1 %copy.5 = f32[384,512]{1,0:T(8,128)} copy(f32[384,512]{1,0:T(8,128)} %shard_map.37) | data formatting | bytes 1572864

commit v4 on v3

--- a/solution.py
+++ b/solution.py
@@ -65,15 +65,6 @@
     lax.fori_loop(1, n, lambda i, _: (record_copy(i).start(), 0)[1], 0)
 
     lax.fori_loop(0, rows // group, arrange, 0)
-    lax.fori_loop(1, n, lambda i, _: (record_arrival(i).wait_recv(), 0)[1], 0)
-
-    for part in range(2):
-        for b in range(slots):
-            piece = rec_all[z + part, :, b * SPAN:(b + 1) * SPAN].astype(jnp.float32)
-            e_mine[part * slots + b:part * slots + b + 1, :] = jnp.sum(piece * piece, axis=0, keepdims=True)
-    energy_copy = pltpu.make_async_remote_copy(
-        src_ref=e_mine, dst_ref=e_sib, send_sem=e_send, recv_sem=e_recv, device_id=other, device_id_type=MESH)
-    energy_copy.start()
 
     row = lax.broadcasted_iota(jnp.int32, (chans, 8, SPAN), 1)
     lane = lax.broadcasted_iota(jnp.int32, (chans, 8, SPAN), 2)
@@ -91,10 +82,10 @@
             y = jnp.where((row & bit) > 0, pltpu.roll(y, SPAN - bit, 2), y)
         return y
 
-    def build(pair, hankel):
+    def build(pair, hankel, pars=(0, 1)):
         raw = [block_at(2 * pair + i) for i in (0, 1, 2, 2)]
         shifted = [shift_rows(raw[i], raw[i + 1]) for i in range(3)]
-        for par in range(2):
+        for par in pars:
             now, after = shifted[par], shifted[par + 1]
             for a in range(0, SPAN // 8, 2):
                 both = []
@@ -134,53 +125,60 @@
 
     def sibling_copy(u):
         return pltpu.make_async_remote_copy(
-            src_ref=acc.at[pl.ds(2 * u, 2)], dst_ref=sib.at[u],
+            src_ref=acc.at[2 * u + 1 - core], dst_ref=sib.at[u],
             send_sem=sib_send.at[u], recv_sem=sib_recv.at[u], device_id=other, device_id_type=MESH)
 
-    def result_copies(u, part):
+    def result_copies(u, part, from_core):
         to = {"tm": u // 2, "chan": home}
-        slot = part * 2 + u % 2
+        block = 2 * (u % 2) + from_core
+        slot = part * 4 + block
         return (
             pltpu.make_async_remote_copy(
-                src_ref=codes.at[u], dst_ref=codes_in.at[part, pl.ds(2 * (u % 2), 2)], send_sem=code_send.at[u],
+                src_ref=codes.at[u], dst_ref=codes_in.at[part, block], send_sem=code_send.at[u],
                 recv_sem=code_recv.at[slot], device_id=to, device_id_type=MESH),
             pltpu.make_async_remote_copy(
-                src_ref=scales.at[u], dst_ref=scales_in.at[part, pl.ds(2 * (u % 2), 2)], send_sem=scale_send.at[u],
+                src_ref=scales.at[u], dst_ref=scales_in.at[part, block], send_sem=scale_send.at[u],
                 recv_sem=scale_recv.at[slot], device_id=to, device_id_type=MESH),
         )
 
-    def hand_over(u):
-        @pl.when(jnp.logical_and(jnp.logical_and(u >= 0, u < 2 * n), lax.rem(u + 2, 2) != core))
-        def _():
-            sibling_copy(u).start()
-
-    def finish(u):
-        @pl.when(jnp.logical_and(jnp.logical_and(u >= 0, u < 2 * n), lax.rem(u + 2, 2) == core))
+    def finish(u, when=True):
+        @pl.when(jnp.logical_and(u >= 0, when))
         def _():
             sibling_copy(u).wait_recv()
             keep = jnp.logical_and(u // 2 == z, core == home)
-            for b in range(2):
-                total = acc[2 * u + b] + sib[u, b]
-                top = jnp.maximum(jnp.max(jnp.abs(total), axis=0, keepdims=True), 1e-37)
-                coded = jnp.round((total * (1.0 / top)) * CODES).astype(jnp.int32).astype(jnp.int16)
-                scale = jnp.broadcast_to(top * (1.0 / CODES), (8, SPAN))
-
-                @pl.when(keep)
-                def _():
-                    codes_in[own_part, 2 * core + b] = coded
-                    scales_in[own_part, 2 * core + b] = scale
-
-                @pl.when(jnp.logical_not(keep))
-                def _():
-                    codes[u, b] = coded
-                    scales[u, b] = scale
+            total = acc[2 * u + core] + sib[u]
+            top = jnp.maximum(jnp.max(jnp.abs(total), axis=0, keepdims=True), 1e-37)
+            coded = jnp.round((total * (1.0 / top)) * CODES).astype(jnp.int32).astype(jnp.int16)
+            scale = jnp.broadcast_to(top * (1.0 / CODES), (8, SPAN))
+
+            @pl.when(keep)
+            def _():
+                codes_in[own_part, 2 * (u % 2) + core] = coded
+                scales_in[own_part, 2 * (u % 2) + core] = scale
 
             @pl.when(jnp.logical_not(keep))
             def _():
-                for copy in result_copies(u, own_part):
+                codes[u] = coded
+                scales[u] = scale
+                for copy in result_copies(u, own_part, core):
                     copy.start()
 
-    build(pair_at(0), ring[0])
+    def begin():
+        build(pair_at(0), ring[0], (0,))
+        build(pair_at(1), ring[1])
+
+    pl.when(upper == 0)(begin)
+    lax.fori_loop(1, n, lambda i, _: (record_arrival(i).wait_recv(), 0)[1], 0)
+    for part in range(2):
+        for b in range(slots):
+            piece = rec_all[z + part, :, b * SPAN:(b + 1) * SPAN].astype(jnp.float32)
+            e_mine[part * slots + b:part * slots + b + 1, :] = jnp.sum(piece * piece, axis=0, keepdims=True)
+    energy_copy = pltpu.make_async_remote_copy(
+        src_ref=e_mine, dst_ref=e_sib, send_sem=e_send, recv_sem=e_recv, device_id=other, device_id_type=MESH)
+    energy_copy.start()
+
+    pl.when(upper == 1)(begin)
+
 
     def step(i, _):
         for r in range(4):
@@ -193,12 +191,20 @@
                 build(following, ring[(r + 1) % 4])
                 multiply(u, ring[r], ring[(r + 3) % 4], ring[(r + 2) % 4])
 
-            @pl.when(jnp.logical_and(u < 0, t + 1 < 2 * n + 2 + 2 * upper))
+            @pl.when(jnp.logical_and(jnp.logical_and(u < 0, t > 0), t + 1 < 2 * n + 2 + 2 * upper))
             def _():
                 build(following, ring[(r + 1) % 4])
 
-            hand_over(u)
-            finish(chunk_at(t - 1))
+            @pl.when(u >= 0)
+            def _():
+                sibling_copy(u).start()
+
+            if r == 2:
+                finish(chunk_at(t - 1))
+            elif r == 3:
+                finish(chunk_at(t - 1))
+            else:
+                finish(chunk_at(t - 1))
         return 0
 
     lax.fori_loop(0, (2 * n + 4) // 4, step, 0)
@@ -217,17 +223,18 @@
         e_mine[b:b + 1, :] = lax.rsqrt(energy / (2 * chans * 4 * SPAN) + 1e-05)
 
     def arrival(i, _):
-        part, from_core = i // 2, i % 2
+        part, block = i // 4, i % 4
+        from_core = block % 2
         source = core * half + part
 
         @pl.when(jnp.logical_not(jnp.logical_and(source == z, from_core == core)))
         def _():
-            for copy in result_copies(from_core, part):
+            for copy in result_copies(block // 2, part, from_core):
                 copy.wait_recv()
 
         return 0
 
-    lax.fori_loop(0, n, arrival, 0)
+    lax.fori_loop(0, 2 * n, arrival, 0)
 
     for slot in range(slots):
         at = span_ref[0, slot]
@@ -239,15 +246,11 @@
             out_ref[part * rows:(part + 1) * rows, slot * SPAN:(slot + 1) * SPAN] = values * scale
 
     def drain(u, _):
-        mine = u % 2 == core
-
-        @pl.when(jnp.logical_not(mine))
+        sibling_copy(u).wait_send()
+
+        @pl.when(jnp.logical_not(jnp.logical_and(u // 2 == z, core == home)))
         def _():
-            sibling_copy(u).wait_send()
-
-        @pl.when(jnp.logical_and(mine, jnp.logical_not(jnp.logical_and(u // 2 == z, core == home))))
-        def _():
-            for copy in result_copies(u, own_part):
+            for copy in result_copies(u, own_part, core):
                 copy.wait_send()
 
         return 0
@@ -275,14 +278,14 @@
             pltpu.VMEM((chans, SPAN, 2 * SPAN), jnp.bfloat16),
             pltpu.VMEM((chans, SPAN, 2 * SPAN), jnp.bfloat16),
             pltpu.VMEM((4 * n, rows, SPAN), jnp.float32),
-            pltpu.VMEM((2 * n, 2, rows, SPAN), jnp.float32),
-            pltpu.VMEM((2 * n, 2, rows, SPAN), jnp.int16),
-            pltpu.VMEM((2 * n, 2, 8, SPAN), jnp.float32),
+            pltpu.VMEM((2 * n, rows, SPAN), jnp.float32),
+            pltpu.VMEM((2 * n, rows, SPAN), jnp.int16),
+            pltpu.VMEM((2 * n, 8, SPAN), jnp.float32),
             pltpu.VMEM((n // 2, 4, rows, SPAN), jnp.int16),
             pltpu.VMEM((n // 2, 4, 8, SPAN), jnp.float32),
             pltpu.VMEM((8, SPAN), jnp.float32),
             pltpu.VMEM((8, SPAN), jnp.float32),
-            dma((n,)), dma((n,)), dma((2 * n,)), dma((2 * n,)), dma((2 * n,)), dma((n,)), dma((2 * n,)), dma((n,)),
+            dma((n,)), dma((n,)), dma((2 * n,)), dma((2 * n,)), dma((2 * n,)), dma((2 * n,)), dma((2 * n,)), dma((2 * n,)),
             dma, dma, dma,
         ],
         compiler_params=pltpu.CompilerParams(collective_id=0, has_side_effects=True, vmem_limit_bytes=62 * 2**20),

time: 30.7 us -> 29.8 us (0.971)
  Pallas kernels: 28.4 us -> 27.5 us
    pallas_call x1, Pallas kernels: 28.4 us -> 27.5 us  [local(): pl.pallas_call(functools.partial(kernel, n, rows, chans, slots), out_shap...]
where the time goes in v4:
time: 29.8 us; the launch traced here: 29.6 us
  Pallas kernels  27.5 us (92%)
  local copies, waits for them, and re-layouts  2.06 us (7%)
    pallas_call x1, Pallas kernels, local(): pl.pallas_call(functools.partial(kernel, n, rows, chans, slots), out_shap...  27.5 us
    unnamed x1, local copies, waits for them, and re-layouts  2.06 us

profile of v4, /device:TPU:0, one launch (start us, length us, event | category | flops | bytes accessed | tf_op | source)
XLA Modules:
  0.0 29.6 jit_solution(4649249292456248620)
XLA Ops:
  0.0 27.5 %shard_map.37 = f32[384,512]{1,0:T(8,128)} custom-call(s32[1,4]{1,0:T(1,128)} %span_ref.1, bf16[16,512]{1,0:T(8,128)(2,1)} %rec_ref.1, bf16[1,192,16,512]{3,2,1,0:T(8,128)(2,1)} %tmpl_ref.1), custom_call_target="tpu_custom_call" | custom-call | tf_op jit(solution)/shard_map/pallas_call | solution.py:267
  27.5 2.1 %copy.5 = f32[384,512]{1,0:T(8,128)} copy(f32[384,512]{1,0:T(8,128)} %shard_map.37) | data formatting | bytes 1572864

commit v5 on v4

--- a/solution.py
+++ b/solution.py
@@ -48,6 +48,7 @@
                 lhs[pl.ds(at, group), c * SPAN:(c + 1) * SPAN] = turned[c]
         return 0
 
+    lax.fori_loop(0, rows // group, arrange, 0)
     pl.semaphore_wait(barrier, 2 * n - 1)
 
     def record_copy(i):
@@ -64,7 +65,6 @@
 
     lax.fori_loop(1, n, lambda i, _: (record_copy(i).start(), 0)[1], 0)
 
-    lax.fori_loop(0, rows // group, arrange, 0)
 
     row = lax.broadcasted_iota(jnp.int32, (chans, 8, SPAN), 1)
     lane = lax.broadcasted_iota(jnp.int32, (chans, 8, SPAN), 2)

time: 29.8 us -> 30.6 us (1.027)
  Pallas kernels: 27.5 us -> 28.3 us
    pallas_call x1, Pallas kernels: 27.5 us -> 28.3 us  [local(): pl.pallas_call(functools.partial(kernel, n, rows, chans, slots), out_shap...]
where the time goes in v5:
time: 30.6 us; the launch traced here: 30.4 us
  Pallas kernels  28.3 us (92%)
  local copies, waits for them, and re-layouts  2.06 us (7%)
    pallas_call x1, Pallas kernels, local(): pl.pallas_call(functools.partial(kernel, n, rows, chans, slots), out_shap...  28.3 us
    unnamed x1, local copies, waits for them, and re-layouts  2.06 us

profile of v5, /device:TPU:0, one launch (start us, length us, event | category | flops | bytes accessed | tf_op | source)
XLA Modules:
  0.0 30.4 jit_solution(5584676306717129395)
XLA Ops:
  0.0 28.3 %shard_map.37 = f32[384,512]{1,0:T(8,128)} custom-call(s32[1,4]{1,0:T(1,128)} %span_ref.1, bf16[16,512]{1,0:T(8,128)(2,1)} %rec_ref.1, bf16[1,192,16,512]{3,2,1,0:T(8,128)(2,1)} %tmpl_ref.1), custom_call_target="tpu_custom_call" | custom-call | tf_op jit(solution)/shard_map/pallas_call | solution.py:267
  28.3 2.1 %copy.5 = f32[384,512]{1,0:T(8,128)} copy(f32[384,512]{1,0:T(8,128)} %shard_map.37) | data formatting | bytes 1572864
